TPU v7x, 32 devices: a whole 2x2x4 slice. The times are simulated.
32 devices in a mesh: virt: 8 (over y, x, core), occ: 4 (over z).
Axes of the slice: x: 2, y: 2, z: 4, core: 2. Of those that a mesh axis runs over, the one named last changes fastest.
Arguments:
- amplitudes: bfloat16 [512, 4096], P('occ', 'virt'), may hold values from -6 to 6
- integrals: bfloat16 [1024, 16384], P(None, 'virt'), may hold values from -0.1875 to 0.1875
- panel_owner: int32 [4, 2], P('occ'), may hold values from 0 to 7, as said below
- inter: bfloat16 [8192, 8192], P('occ', 'virt'), may hold values from -0.125 to 0.125
- dest: int32 [4, 8, 16], P('occ', 'virt'), may hold values from 0 to 3, as said below
- screen: int32 [4, 8, 16], P('occ', 'virt'), may hold values from 0 to 1
Outputs:
- contracted: bfloat16 [512, 8192], P('occ', 'virt')
Inputs may be any that keep to these rules, and one draw needn't show every extreme that they name: `panel_owner`: in each row the 2 entries are distinct. `dest`: among the subtiles of one device that screen marks 1, no two name the same owner.
All inputs are finite; a program needn't handle non-finite values.
Results may differ from a plain program's by a relative error of at most 0.0055.
Values may be sent and summed in bfloat16 or wider, within the bound.
A program may use at most 64 MiB of HBM per device.

v0:
```python
import jax
import jax.numpy as jnp
from jax import lax
from jax.sharding import PartitionSpec as P

SROWS = 32


def on_device(amplitudes, integrals, panel_owner, inter, dest, screen):
    op_rows = amplitudes.shape[0]
    tile = amplitudes.shape[1]
    cols = integrals.shape[1]
    steps = panel_owner.shape[1]
    n_sub = dest.shape[2]
    n_occ = lax.axis_size("occ")
    half_splits = op_rows // SROWS
    col_tiles = cols // tile
    every = lax.all_gather(amplitudes[None], "virt", axis=0, tiled=True)
    chosen_entries = jnp.take(every, panel_owner[0], axis=0)
    chosen_entries = chosen_entries.transpose(1, 0, 2).reshape(op_rows, steps * tile)
    accum = jnp.dot(chosen_entries, integrals, preferred_element_type=jnp.float32)
    ladder = accum.astype(jnp.bfloat16)
    subtiles = (
        ladder.reshape(half_splits, SROWS, col_tiles, tile)
        .transpose(0, 2, 1, 3)
        .reshape(n_sub, SROWS, tile)
    )
    owners = jnp.arange(n_occ, dtype=jnp.int32)
    labels = jnp.arange(1, n_sub + 1, dtype=jnp.int32)
    routing = (dest[0, 0][None, :] == owners[:, None]) & (screen[0, 0][None, :] == 1)
    outgoing = jnp.einsum(
        "os,srt->ort", routing.astype(jnp.bfloat16), subtiles, preferred_element_type=jnp.float32
    ).astype(jnp.bfloat16)
    output_marker = jnp.sum(routing.astype(jnp.int32) * labels[None, :], axis=1).astype(
        jnp.bfloat16
    )[:, None]
    arriving_tiles, tag_in = (
        lax.all_to_all(outgoing, "occ", split_axis=0, concat_axis=0, tiled=True),
        lax.all_to_all(output_marker, "occ", split_axis=0, concat_axis=0, tiled=True),
    )
    choose_surviving = tag_in.astype(jnp.float32) == labels[None, :].astype(jnp.float32)
    summed = jnp.einsum(
        "ez,ead->zad",
        choose_surviving.astype(jnp.bfloat16),
        arriving_tiles,
        preferred_element_type=jnp.float32,
    )
    gathered = summed.astype(jnp.bfloat16)
    left = (
        gathered.reshape(half_splits, col_tiles, SROWS, tile)
        .transpose(0, 2, 1, 3)
        .reshape(op_rows, cols)
    )
    return jnp.dot(left, inter, preferred_element_type=jnp.float32).astype(jnp.bfloat16)


def solution(mesh):
    return jax.shard_map(
        on_device,
        mesh=mesh,
        in_specs=(
            P("occ", "virt"),
            P(None, "virt"),
            P("occ", None),
            P("occ", "virt"),
            P("occ", "virt", None),
            P("occ", "virt", None),
        ),
        out_specs=P("occ", "virt"),
        check_vma=False,
    )
```

profile of v0, /device:TPU:0, one launch (start us, length us, event | category | flops | bytes accessed | tf_op | source)
XLA Modules:
  0.0 64.2 jit_solution(17440745688563391463)
XLA Ops:
  6.5 0.7 %all-gather.3.cloned.1.call-update = ((bf16[128,512]{1,0:T(8,128)(2,1)}), bf16[1024,512]{1,0:T(8,128)(2,1)}) async-update(((), (), s32[]{:S(2)}) %all-gather.3.cloned.1.call-start, bf16[128,512]{1,0:T(8,128)(2,1)} %param.6) | async-update | bytes 1310744
  7.3 0.7 %compare_bitcast_fusion = pred[16]{0:T(512)(128)(4,1)S(1)} fusion(s32[1,1,16]{2,1,0:T(1,128)} %param.11), kind=kLoop, calls=%fused_computation.19 | loop fusion | flops 16 | bytes 80 | tf_op jit(solution)/shard_map/eq | solution.py:30
  7.9 0.8 %select_reduce_fusion = s32[4]{0:T(128)S(1)} fusion(s32[16]{0:T(128)S(1)} %iota_add_fusion, s32[16]{0:T(128)} %bitcast.39, pred[16]{0:T(512)(128)(4,1)S(1)} %compare_bitcast_fusion), kind=kLoop, calls=%fused_computation.12 | loop fusion | flops 252 | bytes 160 | tf_op jit(solution)/shard_map/reduce_sum | solution.py:34
  8.7 0.7 %copy.20 = bf16[4,1,1]{2,1,0:T(2,128)(2,1)} copy(bf16[4,1,1]{0,2,1:T(2,128)(2,1)S(1)} %convert_bitcast_fusion) | data formatting | bytes 16 | tf_op jit(solution)/shard_map/convert_element_type | solution.py:34
  9.4 6.3 %all-to-all-start = ((bf16[4,1,1]{2,1,0:T(2,128)(2,1)}), bf16[4,1,1]{2,1,0:T(2,128)(2,1)S(1)}, u32[]{:S(2)}, u32[]{:S(2)}) async-start(bf16[4,1,1]{2,1,0:T(2,128)(2,1)} %copy.20), calls=%async_computation | async-start | bytes 4096 | tf_op jit(solution)/shard_map/all_to_all | solution.py:39
  15.7 0.7 %fusion.11 = s32[2]{0:T(128)S(1)} fusion(s32[1,2]{1,0:T(1,128)} %param.8), kind=kLoop, calls=%fused_computation.24 | loop fusion | flops 6 | bytes 16 | tf_op jit(solution)/shard_map/jit(_take)/jit(_where)/select_n | solution.py:19
  16.4 0.7 %compare_and_fusion = pred[2]{0:T(512)(128)(4,1)S(1)} fusion(s32[1,2]{1,0:T(1,128)} %param.8), kind=kLoop, calls=%fused_computation.17 | loop fusion | flops 12 | bytes 10 | tf_op jit(solution)/shard_map/jit(_take)/and | solution.py:19
  17.1 18.3 %all-gather.3.cloned.1.call-done = bf16[1024,512]{1,0:T(8,128)(2,1)} async-done(((bf16[128,512]{1,0:T(8,128)(2,1)}), bf16[1024,512]{1,0:T(8,128)(2,1)}) %all-gather.3.cloned.1.call-update) | async-done | bytes 1048592 | tf_op jit(solution)/shard_map/all_gather | solution.py:18
  35.3 1.8 %gather_fusion = bf16[2,128,512]{2,1,0:T(8,128)(2,1)S(1)} fusion(bf16[8,128,512]{2,1,0:T(8,128)(2,1)} %bitcast.38, s32[1024]{0:T(1024)S(1)} %pad_clamp_fusion), kind=kCustom, calls=%fused_computation | custom fusion | bytes 524296 | tf_op jit(solution)/shard_map/jit(_take)/gather | solution.py:19
  37.2 0.1 select_bitcast_fusion
  37.2 0.2 copy.21
  37.4 2.9 %convolution_convert_fusion = bf16[128,2048]{1,0:T(8,128)(2,1)S(1)} fusion(bf16[128,1024]{0,1:T(8,128)(2,1)S(1)} %bitcast.37, bf16[1024,2048]{1,0:T(8,128)(2,1)} %param.7), kind=kOutput, calls=%fused_computation.1 | convolution fusion | flops 537133056 | bytes 4980736 | tf_op jit(solution)/shard_map/dot_general | solution.py:21
  40.4 0.4 reshape.88
  40.7 0.1 copy.22
  40.9 0.4 convolution_convert_fusion.3
  41.3 0.7 %copy.24 = bf16[4,32,512]{2,1,0:T(8,128)(2,1)} copy(bf16[4,32,512]{2,0,1:T(4,128)(2,1)S(1)} %convolution_convert_fusion.3) | data formatting | bytes 262144 | tf_op jit(solution)/shard_map/convert_element_type | solution.py:33
  41.9 4.6 %all-to-all-start.1 = ((bf16[4,32,512]{2,1,0:T(8,128)(2,1)}), bf16[4,32,512]{2,1,0:T(8,128)(2,1)S(1)}, u32[]{:S(2)}, u32[]{:S(2)}) async-start(bf16[4,32,512]{2,1,0:T(8,128)(2,1)} %copy.24), calls=%async_computation.1 | async-start | bytes 262144 | tf_op jit(solution)/shard_map/all_to_all | solution.py:38
  46.6 0.1 convert_reduce_fusion
  46.7 6.2 %all-to-all-done.1 = bf16[4,32,512]{2,1,0:T(8,128)(2,1)S(1)} async-done(((bf16[4,32,512]{2,1,0:T(8,128)(2,1)}), bf16[4,32,512]{2,1,0:T(8,128)(2,1)S(1)}, u32[]{:S(2)}, u32[]{:S(2)}) %all-to-all-start.1) | async-done | bytes 131104 | tf_op jit(solution)/shard_map/all_to_all | solution.py:38
  52.8 0.5 convolution_convert_fusion.1
  53.3 0.1 reshape.90
  53.4 0.2 copy.26
  53.6 0.1 copy.27
  53.7 3.7 %convolution_convert_fusion.2 = bf16[128,1024]{1,0:T(8,128)(2,1)} fusion(bf16[128,2048]{1,0:T(8,128)(2,1)S(1)} %bitcast.34, bf16[2048,1024]{1,0:T(8,128)(2,1)} %param.9), kind=kOutput, calls=%fused_computation.3 | convolution fusion | flops 537001984 | bytes 4980736 | tf_op jit(solution)/shard_map/dot_general | solution.py:54
  (8 shorter events, 0.0 us)
Async XLA Ops:
  6.5 28.8 %all-gather.3.cloned.1.call-start = ((), (), s32[]{:S(2)}) async-start(), calls=%async_computation.2 | async-start | bytes 1179648 | tf_op jit(solution)/shard_map/all_gather | solution.py:18
  9.4 32.5 %all-to-all-start = ((bf16[4,1,1]{2,1,0:T(2,128)(2,1)}), bf16[4,1,1]{2,1,0:T(2,128)(2,1)S(1)}, u32[]{:S(2)}, u32[]{:S(2)}) async-start(bf16[4,1,1]{2,1,0:T(2,128)(2,1)} %copy.20), calls=%async_computation | async-start | bytes 4096 | tf_op jit(solution)/shard_map/all_to_all | solution.py:39
  37.1 3.7 %copy-start = (s32[1,1,16]{2,1,0:T(1,128)S(1)}, s32[1,1,16]{2,1,0:T(1,128)}, u32[]{:S(2)}) copy-start(s32[1,1,16]{2,1,0:T(1,128)} %param.10) | copy-start | bytes 196
  41.9 10.9 %all-to-all-start.1 = ((bf16[4,32,512]{2,1,0:T(8,128)(2,1)}), bf16[4,32,512]{2,1,0:T(8,128)(2,1)S(1)}, u32[]{:S(2)}, u32[]{:S(2)}) async-start(bf16[4,32,512]{2,1,0:T(8,128)(2,1)} %copy.24), calls=%async_computation.1 | async-start | bytes 262144 | tf_op jit(solution)/shard_map/all_to_all | solution.py:38
Sparse Core Ops, SparseCore 0:
  9.2 26.0 all-gather.2
where the time goes:
time: 64.6 us; the launch traced here: 64.2 us
  waiting for transfers between devices  25.2 us (39%)
  between operations  13.5 us (21%)
  starting transfers between devices  11 us (17%)
  matrix products  7.44 us (12%)
  local copies, waits for them, and re-layouts  4.21 us (7%)
  other arithmetic  2.98 us (5%)
    all_gather x1, waiting for transfers between devices, on_device(): every = lax.all_gather(amplitudes[None], 'virt', axis=0, tiled=True)  18.3 us
    all_to_all x1, starting transfers between devices, on_device(): lax.all_to_all(output_marker, 'occ', split_axis=0, concat_axis=0, tiled=T...  6.35 us
    all_to_all x1, waiting for transfers between devices, on_device(): lax.all_to_all(outgoing, 'occ', split_axis=0, concat_axis=0, tiled=True)  6.18 us
    all_to_all x1, starting transfers between devices, on_device(): lax.all_to_all(outgoing, 'occ', split_axis=0, concat_axis=0, tiled=True)  4.6 us
    dot_general x1, matrix products, on_device(): jnp.dot(left, inter, preferred_element_type=jnp.float32)  3.65 us
    dot_general x1, matrix products, on_device(): jnp.dot(chosen_entries, integrals, preferred_element_type=jnp.float32)  2.93 us
    gather x1, local copies, waits for them, and re-layouts, on_device(): chosen_entries = jnp.take(every, panel_owner[0], axis=0)  1.79 us
  transfers between devices with their start and end apart: 3, of which 2 were waited for; matrix products, arithmetic and copies ran while one was open for 16% of the time, Pallas kernels for 0%

commit v1 on v0

v1 whole, which is shorter than its diff:
```python
import functools

import jax
import jax.numpy as jnp
from jax import lax
from jax.experimental import pallas as pl
from jax.experimental.pallas import tpu as pltpu
from jax.sharding import PartitionSpec as P

SROWS = 32
MESH = pl.DeviceIdType.MESH


def flip(index, bit):
    return index + bit * (1 - 2 * lax.rem(lax.div(index, bit), 2))


def peer(me, j, n):
    up = lax.div(me, (n + 1) // 2)
    rising = j + lax.div(j - me + n, n)
    falling = n - 1 - j
    falling = falling - lax.div(me - falling + n, n)
    return up * rising + (1 - up) * falling


def kernel(
    n_virt, n_occ, dims,
    owner_ref, dest_ref, screen_ref, amp_hbm, integ_hbm, inter_hbm,
    out_ref,
    held, integ, inter, route, tables, leaving, arrived, total,
    amp_sem, integ_sem, inter_sem,
    chip_send, chip_recv, pair_send, pair_recv,
    table_send, table_recv, tile_send, tile_recv,
):
    v = lax.axis_index("virt")
    g = lax.axis_index("occ")
    n_chips = n_virt // 2
    chip, core = lax.div(v, 2), lax.rem(v, 2)
    pair = flip(v, 1)
    halves, tile = held.shape[1], held.shape[3]
    steps = owner_ref.shape[1]
    n_sub = dest_ref.shape[2]
    col_tiles = integ.shape[0]

    amp_copy = pltpu.make_async_copy(amp_hbm, held.at[v], amp_sem)
    amp_copy.start()

    barrier = pltpu.get_barrier_semaphore()
    pl.semaphore_signal(barrier, inc=1, device_id={"virt": pair}, device_id_type=MESH)
    for d in range(dims):
        near = flip(chip, 1 << d) * 2 + core
        pl.semaphore_signal(barrier, inc=1, device_id={"virt": near}, device_id_type=MESH)
    for j in range(n_occ - 1):
        pl.semaphore_signal(
            barrier, inc=1, device_id={"occ": peer(g, j, n_occ)}, device_id_type=MESH
        )

    integ_copies, inter_copies = [], []
    for c in range(col_tiles):
        part = integ_hbm.at[:, pl.ds(c * tile, tile)]
        integ_copies.append(pltpu.make_async_copy(part, integ.at[c], integ_sem.at[c]))
        integ_copies[-1].start()
    for c in range(col_tiles):
        part = inter_hbm.at[pl.ds(c * tile, tile)]
        inter_copies.append(pltpu.make_async_copy(part, inter.at[c], inter_sem.at[c]))
        inter_copies[-1].start()

    named = jnp.where(screen_ref[0] == 1, dest_ref[0], -1)
    route[...] = jnp.full(route.shape, -1, jnp.int32)
    route[0:1, 0:n_sub] = named
    label = lax.broadcasted_iota(jnp.int32, (1, n_sub), 1) + 1

    amp_copy.wait()
    pl.semaphore_wait(barrier, 1 + dims + n_occ - 1)

    part_halves = halves // dims

    def chunk(p, rel, bit_core):
        source = chip
        for d in range(dims):
            if rel >> d & 1:
                source = flip(source, 1 << d)
        return held.at[source * 2 + bit_core, pl.ds(p * part_halves, part_halves)]

    def chip_copy(p, rel, d):
        ref = chunk(p, rel, core)
        got = rel ^ (1 << d)
        return pltpu.make_async_remote_copy(
            src_ref=ref, dst_ref=ref,
            send_sem=chip_send.at[p, got], recv_sem=chip_recv.at[p, got],
            device_id={"virt": flip(chip, 1 << d) * 2 + core}, device_id_type=MESH,
        )

    def pair_copy(p, rel):
        ref = chunk(p, rel, core)
        return pltpu.make_async_remote_copy(
            src_ref=ref, dst_ref=ref,
            send_sem=pair_send.at[p, rel], recv_sem=pair_recv.at[p, rel],
            device_id={"virt": pair}, device_id_type=MESH,
        )

    orders = [[(p + t) % dims for t in range(dims)] for p in range(dims)]
    crossing, pairing = {}, {}

    def send_on(p, rel, first):
        for t in range(first, dims):
            d = orders[p][t]
            copy = chip_copy(p, rel, d)
            copy.start()
            crossing[p, rel ^ (1 << d)] = (copy, t + 1)

    for t in range(dims):
        for p in range(dims):
            d = orders[p][t]
            copy = chip_copy(p, 0, d)
            copy.start()
            crossing[p, 1 << d] = (copy, t + 1)
    for p in range(dims):
        pairing[p, 0] = pair_copy(p, 0)
        pairing[p, 0].start()

    table_copies = []
    for j in range(n_occ - 1):
        copy = pltpu.make_async_remote_copy(
            src_ref=route, dst_ref=tables.at[g],
            send_sem=table_send.at[j], recv_sem=table_recv.at[g],
            device_id={"occ": peer(g, j, n_occ)}, device_id_type=MESH,
        )
        copy.start()
        table_copies.append(copy)

    done = set()
    for depth in range(1, dims + 1):
        for p in range(dims):
            for key in [k for k in crossing if k[0] == p and crossing[k][1] == depth and k not in done]:
                copy, after = crossing[key]
                copy.wait_recv()
                done.add(key)
                send_on(key[0], key[1], after)
                pairing[key] = pair_copy(*key)
                pairing[key].start()

    for key in pairing:
        pairing[key].wait_recv()

    for copy in integ_copies:
        copy.wait()

    def made(owner):
        k1 = jnp.sum(jnp.where(named == owner, label, 0))
        k = jnp.maximum(k1 - 1, 0)
        h, c = lax.div(k, col_tiles), lax.rem(k, col_tiles)
        acc = jnp.zeros((SROWS, tile), jnp.float32)
        for s in range(steps):
            left = held[owner_ref[0, s], h]
            right = integ[c, pl.ds(s * tile, tile), :]
            acc += jnp.dot(left, right, preferred_element_type=jnp.float32)
        return jnp.where(k1 > 0, acc, 0.0).astype(jnp.bfloat16)

    tile_copies = []
    for j in range(n_occ - 1):
        owner = peer(g, j, n_occ)
        leaving[j] = made(owner)
        copy = pltpu.make_async_remote_copy(
            src_ref=leaving.at[j], dst_ref=arrived.at[g],
            send_sem=tile_send.at[j], recv_sem=tile_recv.at[g],
            device_id={"occ": owner}, device_id_type=MESH,
        )
        copy.start()
        tile_copies.append(copy)

    for copy in inter_copies:
        copy.wait()

    def add(subtile, table, first):
        k = jnp.maximum(jnp.sum(jnp.where(table == g, label, 0)) - 1, 0)
        h, c = lax.div(k, col_tiles), lax.rem(k, col_tiles)
        part = jnp.dot(subtile, inter[c], preferred_element_type=jnp.float32)
        for i in range(halves):
            rows = pl.ds(i * SROWS, SROWS)
            term = jnp.where(h == i, part, 0.0)
            total[rows] = term if first else total[rows] + term

    add(made(g), named, True)
    for j in reversed(range(n_occ - 1)):
        source = peer(g, j, n_occ)
        pltpu.make_async_remote_copy(
            src_ref=route, dst_ref=tables.at[source],
            send_sem=table_send.at[j], recv_sem=table_recv.at[source],
            device_id={"occ": source}, device_id_type=MESH,
        ).wait_recv()
        pltpu.make_async_remote_copy(
            src_ref=leaving.at[j], dst_ref=arrived.at[source],
            send_sem=tile_send.at[j], recv_sem=tile_recv.at[source],
            device_id={"occ": source}, device_id_type=MESH,
        ).wait_recv()
        add(arrived[source], tables[source, 0:1, 0:n_sub], False)
    out_ref[...] = total[...].astype(out_ref.dtype)

    for key in crossing:
        crossing[key][0].wait_send()
    for key in pairing:
        pairing[key].wait_send()
    for copy in table_copies + tile_copies:
        copy.wait_send()


def solution(mesh):
    n_virt, n_occ = mesh.shape["virt"], mesh.shape["occ"]
    n_chips = n_virt // 2
    dims = n_chips.bit_length() - 1
    assert n_chips == 1 << dims

    def on_device(amplitudes, integrals, panel_owner, inter, dest, screen):
        op_rows, tile = amplitudes.shape
        w_cols = inter.shape[1]
        halves, col_tiles = op_rows // SROWS, integrals.shape[1] // tile
        return pl.pallas_call(
            functools.partial(kernel, n_virt, n_occ, dims),
            out_shape=jax.ShapeDtypeStruct((op_rows, w_cols), jnp.bfloat16),
            in_specs=[
                pl.BlockSpec(memory_space=pltpu.SMEM),
                pl.BlockSpec(memory_space=pltpu.VMEM),
                pl.BlockSpec(memory_space=pltpu.VMEM),
                pl.BlockSpec(memory_space=pl.ANY),
                pl.BlockSpec(memory_space=pl.ANY),
                pl.BlockSpec(memory_space=pl.ANY),
            ],
            out_specs=pl.BlockSpec(memory_space=pltpu.VMEM),
            scratch_shapes=[
                pltpu.VMEM((n_virt, halves, SROWS, tile), jnp.bfloat16),
                pltpu.VMEM((col_tiles, integrals.shape[0], tile), jnp.bfloat16),
                pltpu.VMEM((col_tiles, tile, w_cols), jnp.bfloat16),
                pltpu.VMEM((8, 128), jnp.int32),
                pltpu.VMEM((n_occ, 8, 128), jnp.int32),
                pltpu.VMEM((n_occ, SROWS, tile), jnp.bfloat16),
                pltpu.VMEM((n_occ, SROWS, tile), jnp.bfloat16),
                pltpu.VMEM((op_rows, w_cols), jnp.float32),
                pltpu.SemaphoreType.DMA,
                pltpu.SemaphoreType.DMA((col_tiles,)),
                pltpu.SemaphoreType.DMA((col_tiles,)),
                pltpu.SemaphoreType.DMA((dims, n_chips)),
                pltpu.SemaphoreType.DMA((dims, n_chips)),
                pltpu.SemaphoreType.DMA((dims, n_chips)),
                pltpu.SemaphoreType.DMA((dims, n_chips)),
                pltpu.SemaphoreType.DMA((n_occ,)),
                pltpu.SemaphoreType.DMA((n_occ,)),
                pltpu.SemaphoreType.DMA((n_occ,)),
                pltpu.SemaphoreType.DMA((n_occ,)),
            ],
            compiler_params=pltpu.CompilerParams(collective_id=0, has_side_effects=True),
        )(panel_owner, dest, screen, amplitudes.reshape(halves, SROWS, tile), integrals, inter)

    return jax.shard_map(
        on_device,
        mesh=mesh,
        in_specs=(
            P("occ", "virt"),
            P(None, "virt"),
            P("occ", None),
            P("occ", "virt"),
            P("occ", "virt", None),
            P("occ", "virt", None),
        ),
        out_specs=P("occ", "virt"),
        check_vma=False,
    )
```

time: 64.6 us -> 22.1 us (0.34)
  the two profiles are of different devices: /device:TPU:0 before, /device:TPU:1 now
where the time goes in v1:
time: 22.1 us; the launch traced here: 21.9 us
  Pallas kernels  20.2 us (91%)
  local copies, waits for them, and re-layouts  1.67 us (8%)
    pallas_call x1, Pallas kernels, on_device(): pl.pallas_call(functools.partial(kernel, n_virt, n_occ, dims), out_shape=...  20.2 us
    unnamed x1, local copies, waits for them, and re-layouts  1.67 us

profile of v1, /device:TPU:1, one launch (start us, length us, event | category | flops | bytes accessed | tf_op | source)
XLA Modules:
  0.0 21.9 jit_solution(6208217400029289262)
XLA Ops:
  0.0 20.2 %shard_map.64 = bf16[128,1024]{1,0:T(8,128)(2,1)} custom-call(s32[1,2]{1,0:T(1,128)} %owner_ref.1, s32[1,1,16]{2,1,0:T(1,128)} %dest_ref.1, s32[1,1,16]{2,1,0:T(1,128)} %screen_ref.1, bf16[4,32,512]{2,1,0:T(8,128)(2,1)} %bitcast.1, bf16[1024,2048]{1,0:T(8,128)(2,1)} %integ_hbm.1, bf16[2048,1024]{1,0:T(8,128)(2,1)} %inter_hbm.1), custom_call_target="tpu_custom_call" | custom-call | tf_op jit(solution)/shard_map/pallas_call | solution.py:218
  20.2 1.7 %copy.8 = bf16[128,1024]{1,0:T(8,128)(2,1)} copy(bf16[128,1024]{1,0:T(8,128)(2,1)} %shard_map.64) | data formatting | bytes 524288

commit v2 on v1

--- a/solution.py
+++ b/solution.py
@@ -25,10 +25,10 @@
 
 def kernel(
     n_virt, n_occ, dims,
-    owner_ref, dest_ref, screen_ref, amp_hbm, integ_hbm, inter_hbm,
+    owner_hbm, dest_hbm, screen_hbm, amp_hbm, integ_hbm, inter_hbm,
     out_ref,
-    held, integ, inter, route, tables, leaving, arrived, total,
-    amp_sem, integ_sem, inter_sem,
+    owner_ref, dest_ref, screen_ref, held, integ, inter, route, tables, leaving, arrived, total,
+    small_sem, amp_sem, integ_sem, inter_sem, left_sem, right_sem,
     chip_send, chip_recv, pair_send, pair_recv,
     table_send, table_recv, tile_send, tile_recv,
 ):
@@ -42,18 +42,54 @@
     n_sub = dest_ref.shape[2]
     col_tiles = integ.shape[0]
 
-    amp_copy = pltpu.make_async_copy(amp_hbm, held.at[v], amp_sem)
-    amp_copy.start()
-
     barrier = pltpu.get_barrier_semaphore()
     pl.semaphore_signal(barrier, inc=1, device_id={"virt": pair}, device_id_type=MESH)
     for d in range(dims):
         near = flip(chip, 1 << d) * 2 + core
         pl.semaphore_signal(barrier, inc=1, device_id={"virt": near}, device_id_type=MESH)
-    for j in range(n_occ - 1):
-        pl.semaphore_signal(
-            barrier, inc=1, device_id={"occ": peer(g, j, n_occ)}, device_id_type=MESH
-        )
+
+    def to_right(sem):
+        pl.semaphore_signal(sem, inc=1, device_id={"occ": lax.rem(g + 1, n_occ)}, device_id_type=MESH)
+
+    def to_left(sem):
+        pl.semaphore_signal(sem, inc=1, device_id={"occ": lax.rem(g + n_occ - 1, n_occ)}, device_id_type=MESH)
+
+    @pl.when(g < n_occ - 1)
+    def _():
+        to_right(barrier)
+
+    @pl.when(g > 0)
+    def _():
+        to_left(barrier)
+
+    amp_copy = pltpu.make_async_copy(amp_hbm, held.at[v], amp_sem)
+    amp_copy.start()
+    small_copies = [
+        pltpu.make_async_copy(src, dst, small_sem.at[i])
+        for i, (src, dst) in enumerate(
+            [(dest_hbm, dest_ref), (screen_hbm, screen_ref), (owner_hbm, owner_ref)]
+        )
+    ]
+    for copy in small_copies:
+        copy.start()
+
+    def told_send(r):
+        @pl.when((g >= r - 1) & (g < n_occ - 1))
+        def _():
+            to_right(left_sem)
+
+        @pl.when((g <= n_occ - r) & (g > 0))
+        def _():
+            to_left(right_sem)
+
+    def told_wait(r):
+        @pl.when(g >= r)
+        def _():
+            pl.semaphore_wait(left_sem, 1)
+
+        @pl.when(g <= n_occ - 1 - r)
+        def _():
+            pl.semaphore_wait(right_sem, 1)
 
     integ_copies, inter_copies = [], []
     for c in range(col_tiles):
@@ -65,13 +101,16 @@
         inter_copies.append(pltpu.make_async_copy(part, inter.at[c], inter_sem.at[c]))
         inter_copies[-1].start()
 
+    for copy in small_copies:
+        copy.wait()
     named = jnp.where(screen_ref[0] == 1, dest_ref[0], -1)
     route[...] = jnp.full(route.shape, -1, jnp.int32)
     route[0:1, 0:n_sub] = named
     label = lax.broadcasted_iota(jnp.int32, (1, n_sub), 1) + 1
 
     amp_copy.wait()
-    pl.semaphore_wait(barrier, 1 + dims + n_occ - 1)
+    below, above = lax.div(g + n_occ - 1, n_occ), lax.div(2 * n_occ - 2 - g, n_occ)
+    pl.semaphore_wait(barrier, 1 + dims + below + above)
 
     part_halves = halves // dims
 
@@ -119,18 +158,15 @@
         pairing[p, 0] = pair_copy(p, 0)
         pairing[p, 0].start()
 
-    table_copies = []
-    for j in range(n_occ - 1):
-        copy = pltpu.make_async_remote_copy(
-            src_ref=route, dst_ref=tables.at[g],
-            send_sem=table_send.at[j], recv_sem=table_recv.at[g],
-            device_id={"occ": peer(g, j, n_occ)}, device_id_type=MESH,
-        )
-        copy.start()
-        table_copies.append(copy)
+    if n_occ > 2:
+        told_send(2)
 
     done = set()
     for depth in range(1, dims + 1):
+        if depth == dims:
+            for r in range(2, n_occ - 1):
+                told_wait(r)
+                told_send(r + 1)
         for p in range(dims):
             for key in [k for k in crossing if k[0] == p and crossing[k][1] == depth and k not in done]:
                 copy, after = crossing[key]
@@ -145,6 +181,18 @@
 
     for copy in integ_copies:
         copy.wait()
+    if n_occ > 2:
+        told_wait(n_occ - 1)
+
+    table_copies = []
+    for j in range(n_occ - 1):
+        copy = pltpu.make_async_remote_copy(
+            src_ref=route, dst_ref=tables.at[g],
+            send_sem=table_send.at[j], recv_sem=table_recv.at[g],
+            device_id={"occ": peer(g, j, n_occ)}, device_id_type=MESH,
+        )
+        copy.start()
+        table_copies.append(copy)
 
     def made(owner):
         k1 = jnp.sum(jnp.where(named == owner, label, 0))
@@ -172,16 +220,20 @@
     for copy in inter_copies:
         copy.wait()
 
-    def add(subtile, table, first):
+    def add(subtile, table, first, last):
         k = jnp.maximum(jnp.sum(jnp.where(table == g, label, 0)) - 1, 0)
         h, c = lax.div(k, col_tiles), lax.rem(k, col_tiles)
         part = jnp.dot(subtile, inter[c], preferred_element_type=jnp.float32)
         for i in range(halves):
             rows = pl.ds(i * SROWS, SROWS)
             term = jnp.where(h == i, part, 0.0)
-            total[rows] = term if first else total[rows] + term
-
-    add(made(g), named, True)
+            term = term if first else total[rows] + term
+            if last:
+                out_ref[rows] = term.astype(out_ref.dtype)
+            else:
+                total[rows] = term
+
+    add(made(g), named, True, n_occ == 1)
     for j in reversed(range(n_occ - 1)):
         source = peer(g, j, n_occ)
         pltpu.make_async_remote_copy(
@@ -194,8 +246,7 @@
             send_sem=tile_send.at[j], recv_sem=tile_recv.at[source],
             device_id={"occ": source}, device_id_type=MESH,
         ).wait_recv()
-        add(arrived[source], tables[source, 0:1, 0:n_sub], False)
-    out_ref[...] = total[...].astype(out_ref.dtype)
+        add(arrived[source], tables[source, 0:1, 0:n_sub], False, j == 0)
 
     for key in crossing:
         crossing[key][0].wait_send()
@@ -219,15 +270,13 @@
             functools.partial(kernel, n_virt, n_occ, dims),
             out_shape=jax.ShapeDtypeStruct((op_rows, w_cols), jnp.bfloat16),
             in_specs=[
-                pl.BlockSpec(memory_space=pltpu.SMEM),
-                pl.BlockSpec(memory_space=pltpu.VMEM),
-                pl.BlockSpec(memory_space=pltpu.VMEM),
                 pl.BlockSpec(memory_space=pl.ANY),
-                pl.BlockSpec(memory_space=pl.ANY),
-                pl.BlockSpec(memory_space=pl.ANY),
-            ],
+            ] * 6,
             out_specs=pl.BlockSpec(memory_space=pltpu.VMEM),
             scratch_shapes=[
+                pltpu.SMEM(panel_owner.shape, jnp.int32),
+                pltpu.VMEM(dest.shape, jnp.int32),
+                pltpu.VMEM(screen.shape, jnp.int32),
                 pltpu.VMEM((n_virt, halves, SROWS, tile), jnp.bfloat16),
                 pltpu.VMEM((col_tiles, integrals.shape[0], tile), jnp.bfloat16),
                 pltpu.VMEM((col_tiles, tile, w_cols), jnp.bfloat16),
@@ -236,9 +285,12 @@
                 pltpu.VMEM((n_occ, SROWS, tile), jnp.bfloat16),
                 pltpu.VMEM((n_occ, SROWS, tile), jnp.bfloat16),
                 pltpu.VMEM((op_rows, w_cols), jnp.float32),
+                pltpu.SemaphoreType.DMA((3,)),
                 pltpu.SemaphoreType.DMA,
                 pltpu.SemaphoreType.DMA((col_tiles,)),
                 pltpu.SemaphoreType.DMA((col_tiles,)),
+                pltpu.SemaphoreType.REGULAR,
+                pltpu.SemaphoreType.REGULAR,
                 pltpu.SemaphoreType.DMA((dims, n_chips)),
                 pltpu.SemaphoreType.DMA((dims, n_chips)),
                 pltpu.SemaphoreType.DMA((dims, n_chips)),
@@ -248,8 +300,8 @@
                 pltpu.SemaphoreType.DMA((n_occ,)),
                 pltpu.SemaphoreType.DMA((n_occ,)),
             ],
-            compiler_params=pltpu.CompilerParams(collective_id=0, has_side_effects=True),
-        )(panel_owner, dest, screen, amplitudes.reshape(halves, SROWS, tile), integrals, inter)
+            compiler_params=pltpu.CompilerParams(collective_id=0, has_side_effects=True, vmem_limit_bytes=24 << 20),
+        )(*[pltpu.with_memory_space_constraint(x, pltpu.HBM) for x in (panel_owner, dest, screen, amplitudes.reshape(halves, SROWS, tile), integrals, inter)])
 
     return jax.shard_map(
         on_device,

time: 22.1 us -> 21 us (0.950)
  local copies, waits for them, and re-layouts: 1.67 us -> 0.71 us
    unnamed x1, local copies, waits for them, and re-layouts: 1.67 us -> 0.71 us
where the time goes in v2:
time: 21 us; the launch traced here: 20.9 us
  Pallas kernels  20.1 us (96%)
  local copies, waits for them, and re-layouts  0.71 us (3%)
    pallas_call x1, Pallas kernels, on_device(): pl.pallas_call(functools.partial(kernel, n_virt, n_occ, dims), out_shape=...  20.1 us
    unnamed x1, local copies, waits for them, and re-layouts  0.71 us

profile of v2, /device:TPU:1, one launch (start us, length us, event | category | flops | bytes accessed | tf_op | source)
XLA Modules:
  0.0 20.9 jit_solution(6242615056501777152)
XLA Ops:
  0.0 20.1 %shard_map.64 = bf16[128,1024]{1,0:T(8,128)(2,1)S(1)} custom-call(s32[1,2]{1,0:T(1,128)} %owner_hbm.1, s32[1,1,16]{2,1,0:T(1,128)} %dest_hbm.1, s32[1,1,16]{2,1,0:T(1,128)} %screen_hbm.1, bf16[4,32,512]{2,1,0:T(8,128)(2,1)} %bitcast.1, bf16[1024,2048]{1,0:T(8,128)(2,1)} %integ_hbm.1, bf16[2048,1024]{1,0:T(8,128)(2,1)} %inter_hbm.1), custom_call_target="tpu_custom_call" | custom-call | tf_op jit(solution)/shard_map/pallas_call | solution.py:269
  20.2 0.7 %copy.8 = bf16[128,1024]{1,0:T(8,128)(2,1)} copy(bf16[128,1024]{1,0:T(8,128)(2,1)S(1)} %shard_map.64) | data formatting | bytes 524288

commit v3 on v2

--- a/solution.py
+++ b/solution.py
@@ -96,10 +96,6 @@
         part = integ_hbm.at[:, pl.ds(c * tile, tile)]
         integ_copies.append(pltpu.make_async_copy(part, integ.at[c], integ_sem.at[c]))
         integ_copies[-1].start()
-    for c in range(col_tiles):
-        part = inter_hbm.at[pl.ds(c * tile, tile)]
-        inter_copies.append(pltpu.make_async_copy(part, inter.at[c], inter_sem.at[c]))
-        inter_copies[-1].start()
 
     for copy in small_copies:
         copy.wait()
@@ -112,7 +108,8 @@
     below, above = lax.div(g + n_occ - 1, n_occ), lax.div(2 * n_occ - 2 - g, n_occ)
     pl.semaphore_wait(barrier, 1 + dims + below + above)
 
-    part_halves = halves // dims
+    parts = chip_recv.shape[0]
+    part_halves = halves // parts
 
     def chunk(p, rel, bit_core):
         source = chip
@@ -138,7 +135,7 @@
             device_id={"virt": pair}, device_id_type=MESH,
         )
 
-    orders = [[(p + t) % dims for t in range(dims)] for p in range(dims)]
+    orders = [[(p + t) % dims for t in range(dims)] for p in range(parts)]
     crossing, pairing = {}, {}
 
     def send_on(p, rel, first):
@@ -149,32 +146,34 @@
             crossing[p, rel ^ (1 << d)] = (copy, t + 1)
 
     for t in range(dims):
-        for p in range(dims):
+        for p in range(parts):
             d = orders[p][t]
             copy = chip_copy(p, 0, d)
             copy.start()
             crossing[p, 1 << d] = (copy, t + 1)
-    for p in range(dims):
+    for p in range(parts):
         pairing[p, 0] = pair_copy(p, 0)
         pairing[p, 0].start()
 
     if n_occ > 2:
         told_send(2)
-
-    done = set()
+    for c in range(col_tiles):
+        part = inter_hbm.at[pl.ds(c * tile, tile)]
+        inter_copies.append(pltpu.make_async_copy(part, inter.at[c], inter_sem.at[c]))
+        inter_copies[-1].start()
+
     for depth in range(1, dims + 1):
         if depth == dims:
             for r in range(2, n_occ - 1):
                 told_wait(r)
                 told_send(r + 1)
-        for p in range(dims):
-            for key in [k for k in crossing if k[0] == p and crossing[k][1] == depth and k not in done]:
-                copy, after = crossing[key]
-                copy.wait_recv()
-                done.add(key)
-                send_on(key[0], key[1], after)
-                pairing[key] = pair_copy(*key)
-                pairing[key].start()
+        keys = [k for k in crossing if crossing[k][1] == depth]
+        for key in sorted(keys, key=lambda k: (bin(k[1]).count("1"), k)):
+            copy, after = crossing[key]
+            copy.wait_recv()
+            send_on(key[0], key[1], after)
+            pairing[key] = pair_copy(*key)
+            pairing[key].start()
 
     for key in pairing:
         pairing[key].wait_recv()
@@ -266,6 +265,7 @@
         op_rows, tile = amplitudes.shape
         w_cols = inter.shape[1]
         halves, col_tiles = op_rows // SROWS, integrals.shape[1] // tile
+        parts = halves if halves % dims == 0 else dims
         return pl.pallas_call(
             functools.partial(kernel, n_virt, n_occ, dims),
             out_shape=jax.ShapeDtypeStruct((op_rows, w_cols), jnp.bfloat16),
@@ -291,10 +291,10 @@
                 pltpu.SemaphoreType.DMA((col_tiles,)),
                 pltpu.SemaphoreType.REGULAR,
                 pltpu.SemaphoreType.REGULAR,
-                pltpu.SemaphoreType.DMA((dims, n_chips)),
-                pltpu.SemaphoreType.DMA((dims, n_chips)),
-                pltpu.SemaphoreType.DMA((dims, n_chips)),
-                pltpu.SemaphoreType.DMA((dims, n_chips)),
+                pltpu.SemaphoreType.DMA((parts, n_chips)),
+                pltpu.SemaphoreType.DMA((parts, n_chips)),
+                pltpu.SemaphoreType.DMA((parts, n_chips)),
+                pltpu.SemaphoreType.DMA((parts, n_chips)),
                 pltpu.SemaphoreType.DMA((n_occ,)),
                 pltpu.SemaphoreType.DMA((n_occ,)),
                 pltpu.SemaphoreType.DMA((n_occ,)),

time: 21 us -> 20.2 us (0.962)
  Pallas kernels: 20.1 us -> 19.4 us
    pallas_call x1, Pallas kernels: 20.1 us -> 19.4 us  [on_device(): pl.pallas_call(functools.partial(kernel, n_virt, n_occ, dims), out_shape=...]
where the time goes in v3:
time: 20.2 us; the launch traced here: 20.1 us
  Pallas kernels  19.4 us (96%)
  local copies, waits for them, and re-layouts  0.71 us (4%)
    pallas_call x1, Pallas kernels, on_device(): pl.pallas_call(functools.partial(kernel, n_virt, n_occ, dims), out_shape=...  19.4 us
    unnamed x1, local copies, waits for them, and re-layouts  0.71 us

profile of v3, /device:TPU:1, one launch (start us, length us, event | category | flops | bytes accessed | tf_op | source)
XLA Modules:
  0.0 20.1 jit_solution(18146817079846045015)
XLA Ops:
  0.0 19.4 %shard_map.64 = bf16[128,1024]{1,0:T(8,128)(2,1)S(1)} custom-call(s32[1,2]{1,0:T(1,128)} %owner_hbm.1, s32[1,1,16]{2,1,0:T(1,128)} %dest_hbm.1, s32[1,1,16]{2,1,0:T(1,128)} %screen_hbm.1, bf16[4,32,512]{2,1,0:T(8,128)(2,1)} %bitcast.1, bf16[1024,2048]{1,0:T(8,128)(2,1)} %integ_hbm.1, bf16[2048,1024]{1,0:T(8,128)(2,1)} %inter_hbm.1), custom_call_target="tpu_custom_call" | custom-call | tf_op jit(solution)/shard_map/pallas_call | solution.py:269
  19.4 0.7 %copy.8 = bf16[128,1024]{1,0:T(8,128)(2,1)} copy(bf16[128,1024]{1,0:T(8,128)(2,1)S(1)} %shard_map.64) | data formatting | bytes 524288

commit v4 on v3

--- a/solution.py
+++ b/solution.py
@@ -64,14 +64,6 @@
 
     amp_copy = pltpu.make_async_copy(amp_hbm, held.at[v], amp_sem)
     amp_copy.start()
-    small_copies = [
-        pltpu.make_async_copy(src, dst, small_sem.at[i])
-        for i, (src, dst) in enumerate(
-            [(dest_hbm, dest_ref), (screen_hbm, screen_ref), (owner_hbm, owner_ref)]
-        )
-    ]
-    for copy in small_copies:
-        copy.start()
 
     def told_send(r):
         @pl.when((g >= r - 1) & (g < n_occ - 1))
@@ -92,17 +84,6 @@
             pl.semaphore_wait(right_sem, 1)
 
     integ_copies, inter_copies = [], []
-    for c in range(col_tiles):
-        part = integ_hbm.at[:, pl.ds(c * tile, tile)]
-        integ_copies.append(pltpu.make_async_copy(part, integ.at[c], integ_sem.at[c]))
-        integ_copies[-1].start()
-
-    for copy in small_copies:
-        copy.wait()
-    named = jnp.where(screen_ref[0] == 1, dest_ref[0], -1)
-    route[...] = jnp.full(route.shape, -1, jnp.int32)
-    route[0:1, 0:n_sub] = named
-    label = lax.broadcasted_iota(jnp.int32, (1, n_sub), 1) + 1
 
     amp_copy.wait()
     below, above = lax.div(g + n_occ - 1, n_occ), lax.div(2 * n_occ - 2 - g, n_occ)
@@ -157,10 +138,29 @@
 
     if n_occ > 2:
         told_send(2)
+    small_copies = [
+        pltpu.make_async_copy(src, dst, small_sem.at[i])
+        for i, (src, dst) in enumerate(
+            [(dest_hbm, dest_ref), (screen_hbm, screen_ref), (owner_hbm, owner_ref)]
+        )
+    ]
+    for copy in small_copies:
+        copy.start()
+    for c in range(col_tiles):
+        part = integ_hbm.at[:, pl.ds(c * tile, tile)]
+        integ_copies.append(pltpu.make_async_copy(part, integ.at[c], integ_sem.at[c]))
+        integ_copies[-1].start()
     for c in range(col_tiles):
         part = inter_hbm.at[pl.ds(c * tile, tile)]
         inter_copies.append(pltpu.make_async_copy(part, inter.at[c], inter_sem.at[c]))
         inter_copies[-1].start()
+
+    for copy in small_copies:
+        copy.wait()
+    named = jnp.where(screen_ref[0] == 1, dest_ref[0], -1)
+    route[...] = jnp.full(route.shape, -1, jnp.int32)
+    route[0:1, 0:n_sub] = named
+    label = lax.broadcasted_iota(jnp.int32, (1, n_sub), 1) + 1
 
     for depth in range(1, dims + 1):
         if depth == dims:

time: 20.2 us -> 19.8 us (0.980)
  Pallas kernels: 19.4 us -> 18.9 us
    pallas_call x1, Pallas kernels: 19.4 us -> 18.9 us  [on_device(): pl.pallas_call(functools.partial(kernel, n_virt, n_occ, dims), out_shape=...]
where the time goes in v4:
time: 19.8 us; the launch traced here: 19.7 us
  Pallas kernels  18.9 us (95%)
  local copies, waits for them, and re-layouts  0.71 us (4%)
    pallas_call x1, Pallas kernels, on_device(): pl.pallas_call(functools.partial(kernel, n_virt, n_occ, dims), out_shape=...  18.9 us
    unnamed x1, local copies, waits for them, and re-layouts  0.71 us

profile of v4, /device:TPU:1, one launch (start us, length us, event | category | flops | bytes accessed | tf_op | source)
XLA Modules:
  0.0 19.7 jit_solution(6350165929187603021)
XLA Ops:
  0.0 18.9 %shard_map.64 = bf16[128,1024]{1,0:T(8,128)(2,1)S(1)} custom-call(s32[1,2]{1,0:T(1,128)} %owner_hbm.1, s32[1,1,16]{2,1,0:T(1,128)} %dest_hbm.1, s32[1,1,16]{2,1,0:T(1,128)} %screen_hbm.1, bf16[4,32,512]{2,1,0:T(8,128)(2,1)} %bitcast.1, bf16[1024,2048]{1,0:T(8,128)(2,1)} %integ_hbm.1, bf16[2048,1024]{1,0:T(8,128)(2,1)} %inter_hbm.1), custom_call_target="tpu_custom_call" | custom-call | tf_op jit(solution)/shard_map/pallas_call | solution.py:269
  18.9 0.7 %copy.8 = bf16[128,1024]{1,0:T(8,128)(2,1)} copy(bf16[128,1024]{1,0:T(8,128)(2,1)S(1)} %shard_map.64) | data formatting | bytes 524288

commit v5 on v4

--- a/solution.py
+++ b/solution.py
@@ -162,6 +162,12 @@
     route[0:1, 0:n_sub] = named
     label = lax.broadcasted_iota(jnp.int32, (1, n_sub), 1) + 1
 
+    def label_for(table, owner):
+        return jnp.sum(jnp.where(table == owner, label, 0))
+
+    others = [label_for(named, peer(g, j, n_occ)) for j in range(n_occ - 1)]
+    mine = label_for(named, g)
+
     for depth in range(1, dims + 1):
         if depth == dims:
             for r in range(2, n_occ - 1):
@@ -193,8 +199,7 @@
         copy.start()
         table_copies.append(copy)
 
-    def made(owner):
-        k1 = jnp.sum(jnp.where(named == owner, label, 0))
+    def made(k1):
         k = jnp.maximum(k1 - 1, 0)
         h, c = lax.div(k, col_tiles), lax.rem(k, col_tiles)
         acc = jnp.zeros((SROWS, tile), jnp.float32)
@@ -207,7 +212,7 @@
     tile_copies = []
     for j in range(n_occ - 1):
         owner = peer(g, j, n_occ)
-        leaving[j] = made(owner)
+        leaving[j] = made(others[j])
         copy = pltpu.make_async_remote_copy(
             src_ref=leaving.at[j], dst_ref=arrived.at[g],
             send_sem=tile_send.at[j], recv_sem=tile_recv.at[g],
@@ -219,8 +224,8 @@
     for copy in inter_copies:
         copy.wait()
 
-    def add(subtile, table, first, last):
-        k = jnp.maximum(jnp.sum(jnp.where(table == g, label, 0)) - 1, 0)
+    def add(subtile, k1, first, last):
+        k = jnp.maximum(k1 - 1, 0)
         h, c = lax.div(k, col_tiles), lax.rem(k, col_tiles)
         part = jnp.dot(subtile, inter[c], preferred_element_type=jnp.float32)
         for i in range(halves):
@@ -232,7 +237,7 @@
             else:
                 total[rows] = term
 
-    add(made(g), named, True, n_occ == 1)
+    add(made(mine), mine, True, n_occ == 1)
     for j in reversed(range(n_occ - 1)):
         source = peer(g, j, n_occ)
         pltpu.make_async_remote_copy(
@@ -240,12 +245,13 @@
             send_sem=table_send.at[j], recv_sem=table_recv.at[source],
             device_id={"occ": source}, device_id_type=MESH,
         ).wait_recv()
+        k1 = label_for(tables[source, 0:1, 0:n_sub], g)
         pltpu.make_async_remote_copy(
             src_ref=leaving.at[j], dst_ref=arrived.at[source],
             send_sem=tile_send.at[j], recv_sem=tile_recv.at[source],
             device_id={"occ": source}, device_id_type=MESH,
         ).wait_recv()
-        add(arrived[source], tables[source, 0:1, 0:n_sub], False, j == 0)
+        add(arrived[source], k1, False, j == 0)
 
     for key in crossing:
         crossing[key][0].wait_send()

time: 19.8 us -> 19.5 us (0.985)
  Pallas kernels: 18.9 us -> 18.6 us
    pallas_call x1, Pallas kernels: 18.9 us -> 18.6 us  [on_device(): pl.pallas_call(functools.partial(kernel, n_virt, n_occ, dims), out_shape=...]
where the time goes in v5:
time: 19.5 us; the launch traced here: 19.3 us
  Pallas kernels  18.6 us (95%)
  local copies, waits for them, and re-layouts  0.71 us (4%)
    pallas_call x1, Pallas kernels, on_device(): pl.pallas_call(functools.partial(kernel, n_virt, n_occ, dims), out_shape=...  18.6 us
    unnamed x1, local copies, waits for them, and re-layouts  0.71 us

profile of v5, /device:TPU:1, one launch (start us, length us, event | category | flops | bytes accessed | tf_op | source)
XLA Modules:
  0.0 19.3 jit_solution(3118976049174065110)
XLA Ops:
  0.0 18.6 %shard_map.64 = bf16[128,1024]{1,0:T(8,128)(2,1)S(1)} custom-call(s32[1,2]{1,0:T(1,128)} %owner_hbm.1, s32[1,1,16]{2,1,0:T(1,128)} %dest_hbm.1, s32[1,1,16]{2,1,0:T(1,128)} %screen_hbm.1, bf16[4,32,512]{2,1,0:T(8,128)(2,1)} %bitcast.1, bf16[1024,2048]{1,0:T(8,128)(2,1)} %integ_hbm.1, bf16[2048,1024]{1,0:T(8,128)(2,1)} %inter_hbm.1), custom_call_target="tpu_custom_call" | custom-call | tf_op jit(solution)/shard_map/pallas_call | solution.py:275
  18.6 0.7 %copy.8 = bf16[128,1024]{1,0:T(8,128)(2,1)} copy(bf16[128,1024]{1,0:T(8,128)(2,1)S(1)} %shard_map.64) | data formatting | bytes 524288
